TPU v7x, 256 devices: a whole 4x4x8 slice. The times are simulated.
256 devices in a mesh: wide: 128 (over x, y, z_lo, core), head: 2 (over z_hi).
Axes of the slice: x: 4, y: 4, z: 8 (z_hi: 2, z_lo: 4; z = z_hi * 4 + z_lo), core: 2. Of those that a mesh axis runs over, the one named last changes fastest.
Arguments:
- branch_query: bfloat16 [512, 8192], P('wide', 'head'), may hold values from -6 to 6
- key_new: bfloat16 [512, 1024], P('wide', 'head'), may hold values from -6 to 6
- value_new: bfloat16 [512, 1024], P('wide', 'head'), may hold values from -6 to 6
- pool_pages: bfloat16 [2, 8192, 16, 1024], P(None, 'wide', None, 'head'), may hold values from -6 to 6
- page_table: int32 [512, 16], P('wide'), may hold values from 0 to 63, as said below
- tail_length: int32 [512], P('wide'), may hold values from 1 to 256
- parent_row: int32 [512], P('wide'), may hold values from 0 to 511, as said below
- residual: bfloat16 [512, 8192], P(('wide', 'head')), may hold values from -6 to 6
- norm_gain: float32 [8192], replicated, may hold values from 0.5 to 1.5
- gate_blocks: bfloat16 [128, 32, 128, 128], P('wide'), may hold values from -0.09375 to 0.09375
- up_blocks: bfloat16 [128, 32, 128, 128], P('wide'), may hold values from -0.09375 to 0.09375
- gate_up_keep: int32 [128, 32], P('wide'), may hold values from 0 to 63, as said below
- gate_scale: float32 [128, 32], P('wide'), may hold values from 0.5 to 2
- up_scale: float32 [128, 32], P('wide'), may hold values from 0.5 to 2
- down_blocks: bfloat16 [128, 32, 128, 128], P('wide'), may hold values from -0.0625 to 0.0625
- down_keep: int32 [128, 32], P('wide'), may hold values from 0 to 63, as said below
- down_scale: float32 [128, 32], P('wide'), may hold values from 0.5 to 2
Outputs:
- layer_out: bfloat16 [512, 8192], P(('wide', 'head'))
Inputs may be any that keep to these rules, and one draw needn't show every extreme that they name: parent_row never falls with the branch index, and parent_row[b] <= b and parent_row[b] > b - 4. `page_table`: the entries of the 4 rows held by one index of wide name each of that index's 64 pages once. `gate_up_keep`: each row names 32 different blocks. `down_keep`: each row names 32 different blocks.
All inputs are finite; a program needn't handle non-finite values.
Results may differ from a plain program's by a relative error of at most 0.017.
Values may be sent and summed in bfloat16 or wider, within the bound.
A program may use at most 64 MiB of HBM per device.

v0:
```python
import math
import jax
import jax.numpy as jnp
from jax import lax
from jax.sharding import PartitionSpec as P

HD = 128
BLK = 128


def shifted(block, axis, distance):
    devices = range(lax.axis_size(axis))
    route = [(i - distance, i) for i in devices if i - distance in devices]
    return lax.ppermute(block, axis, route)


def attend(branch_query, key_new, value_new, child_tails, child_length):
    row_count = branch_query.shape[0]
    groups = key_new.shape[1] // HD
    per_group = branch_query.shape[1] // (groups * HD)
    tail_size = child_tails.shape[2]
    queries = branch_query.reshape(row_count, groups, per_group, HD)
    tail_keys = child_tails[0].reshape(row_count, tail_size, groups, HD)
    tail_values = child_tails[1].reshape(row_count, tail_size, groups, HD)
    own_keys = key_new.reshape(row_count, groups, HD)
    own_values = value_new.reshape(row_count, groups, HD)
    factor = 1.0 / math.sqrt(HD)
    tail_scores = (
        jnp.einsum("rgjd,rtgd->rgjt", queries, tail_keys, preferred_element_type=jnp.float32)
        * factor
    )
    own_scores = (
        jnp.einsum("rgjd,rgd->rgj", queries, own_keys, preferred_element_type=jnp.float32) * factor
    )
    live_mask = (jnp.arange(tail_size, dtype=jnp.float32)[None, :] < child_length[:, None])[
        :, None, None, :
    ]
    top_score = jnp.maximum(jnp.max(jnp.where(live_mask, tail_scores, -1e30), axis=-1), own_scores)
    tail_exp = jnp.where(live_mask, jnp.exp(tail_scores - top_score[..., None]), 0.0)
    own_exp = jnp.exp(own_scores - top_score)
    totals = jnp.sum(tail_exp, axis=-1) + own_exp
    tail_weights = (tail_exp / totals[..., None]).astype(jnp.bfloat16)
    own_weights = (own_exp / totals).astype(jnp.bfloat16)
    mixture = jnp.einsum(
        "rgjt,rtgd->rgjd", tail_weights, tail_values, preferred_element_type=jnp.float32
    )
    mixture = mixture + own_weights[..., None].astype(jnp.float32) * own_values[
        :, :, None, :
    ].astype(jnp.float32)
    return mixture.reshape(row_count, -1).astype(jnp.bfloat16)


def ffn_terms(picked, gate_blocks, up_blocks, gate_scale, up_scale, down_blocks, down_scale):
    gate_part = jnp.einsum(
        "rkd,kdf->rkf", picked, gate_blocks[0], preferred_element_type=jnp.float32
    )
    up_part = jnp.einsum("rkd,kdf->rkf", picked, up_blocks[0], preferred_element_type=jnp.float32)
    gate_sum = jnp.sum(gate_part * gate_scale[0][None, :, None], axis=1)
    up_sum = jnp.sum(up_part * up_scale[0][None, :, None], axis=1)
    hidden = (jax.nn.silu(gate_sum) * up_sum).astype(jnp.bfloat16)
    return (
        jnp.einsum("rf,kfe->rke", hidden, down_blocks[0], preferred_element_type=jnp.float32)
        * down_scale[0][None, :, None]
    )


def per_device(
    branch_query,
    key_new,
    value_new,
    pool_pages,
    page_table,
    tail_length,
    parent_row,
    residual,
    norm_gain,
    gate_blocks,
    up_blocks,
    gate_up_keep,
    gate_scale,
    up_scale,
    down_blocks,
    down_keep,
    down_scale,
):
    row_count = branch_query.shape[0]
    tail_size = page_table.shape[1] * pool_pages.shape[2]
    own_tails = pool_pages[:, page_table].reshape(2, row_count, tail_size, pool_pages.shape[3])
    own_length = tail_length.astype(jnp.bfloat16)
    prior_tails, prior_length = shifted((own_tails, own_length), "wide", 1)
    both_tails = jnp.concatenate([prior_tails, own_tails], axis=1)
    both_length = jnp.concatenate([prior_length, own_length]).astype(jnp.float32)
    local_parent = parent_row - (lax.axis_index("wide") - 1) * row_count
    child_tails = both_tails[:, local_parent]
    child_length = both_length[local_parent]
    attention = attend(branch_query, key_new, value_new, child_tails, child_length)
    head_rows = lax.all_to_all(attention, "head", split_axis=0, concat_axis=1, tiled=True)
    middle = residual.astype(jnp.float32) + head_rows.astype(jnp.float32)
    normed = (
        middle * lax.rsqrt(jnp.mean(middle * middle, axis=-1, keepdims=True) + 1e-05) * norm_gain
    ).astype(jnp.bfloat16)
    keep_lists = lax.all_gather(
        jnp.concatenate([gate_up_keep, down_keep], axis=1), "wide", axis=0, tiled=True
    )
    keep = gate_up_keep.shape[1]
    in_keep, out_keep = (keep_lists[:, :keep], keep_lists[:, keep:])
    feature_blocks = normed.shape[1] // BLK
    normed_blocks = normed.reshape(normed.shape[0], feature_blocks, BLK)
    outgoing = jnp.swapaxes(normed_blocks[:, in_keep], 0, 1)
    picked = lax.all_to_all(outgoing, "wide", split_axis=0, concat_axis=0, tiled=True)
    picked = picked.reshape(-1, keep, BLK)
    contrib = ffn_terms(
        picked, gate_blocks, up_blocks, gate_scale, up_scale, down_blocks, down_scale
    ).astype(jnp.bfloat16)
    contrib = contrib.reshape(-1, normed.shape[0], keep, BLK)
    arrived = lax.all_to_all(contrib, "wide", split_axis=0, concat_axis=0, tiled=True)
    senders = arrived.shape[0]
    placement = (
        out_keep.reshape(senders * keep, 1) == jnp.arange(feature_blocks, dtype=jnp.int32)[None, :]
    ).astype(jnp.bfloat16)
    flat = jnp.swapaxes(arrived, 0, 1).reshape(normed.shape[0], senders * keep, BLK)
    ffn_share = jnp.einsum(
        "rsd,sb->rbd", flat, placement, preferred_element_type=jnp.float32
    ).reshape(normed.shape[0], -1)
    return (middle + ffn_share).astype(jnp.bfloat16)


def solution(mesh):
    placed = (
        P("wide", "head"),
        P("wide", "head"),
        P("wide", "head"),
        P(None, "wide", None, "head"),
        P("wide", None),
        P("wide"),
        P("wide"),
        P(("wide", "head"), None),
        P(),
        P("wide", None, None, None),
        P("wide", None, None, None),
        P("wide", None),
        P("wide", None),
        P("wide", None),
        P("wide", None, None, None),
        P("wide", None),
        P("wide", None),
    )
    return jax.shard_map(
        per_device, mesh=mesh, in_specs=placed, out_specs=P(("wide", "head"), None), check_vma=False
    )
```

profile of v0, /device:TPU:1, one launch (start us, length us, event | category | flops | bytes accessed | tf_op | source)
XLA Modules:
  0.0 395.7 jit_solution(13125555480860348929)
XLA Ops:
  0.0 0.8 compare_select_fusion.1
  0.8 0.1 reshape.96
  0.9 0.7 copy-done
  1.6 2.0 gather_fusion.1
  3.6 0.0 copy-start.12
  3.6 0.0 copy-start.13
  3.7 3.2 copy.29
  6.8 4.9 %collective-permute-start.1 = (bf16[2,4,256,512]{3,2,1,0:T(8,128)(2,1)}, bf16[2,4,256,512]{3,2,1,0:T(8,128)(2,1)}, u32[]{:S(2)}, u32[]{:S(2)}) collective-permute-start(bf16[2,4,256,512]{3,2,1,0:T(8,128)(2,1)} %bitcast.2), channel_id=1, source_target_pairs={{0,2},{2,4},{4,6},{6,8},{8,10},{10,12},{12,14},{14,16},{16,18},{18... | collective-permute-start | bytes 6291464 | tf_op jit(solution)/shard_map/ppermute | solution.py:14
  11.8 1.9 collective-permute-start
  13.8 0.1 add_bitcast_fusion
  13.9 191.1 %all-gather = s32[128,1,64]{2,1,0:T(1,128)S(1)} all-gather(s32[1,1,64]{2,1,0:T(1,128)S(1)} %add_bitcast_fusion), channel_id=1, replica_groups=mesh['wide'=128,'head'=2] {'wide'}, dimensions={0}, use_global_device_ids=true | all-gather | bytes 33024 | tf_op jit(solution)/shard_map/all_gather | solution.py:102
  204.9 0.1 fusion.26
  205.0 0.1 reshape.112
  205.2 0.1 fusion.15
  205.3 0.1 maximum_convert_fusion
  205.4 0.6 gather_fusion
  206.0 0.1 iota_compare_fusion.1
  206.1 4.5 %pad_maximum_fusion = bf16[2,8,256,512]{3,2,1,0:T(8,128)(2,1)} fusion(bf16[2,4,256,512]{3,2,1,0:T(8,128)(2,1)} %bitcast.2, bf16[2,4,256,512]{3,2,1,0:T(8,128)(2,1)} %collective-permute-done.1), kind=kLoop, calls=%fused_computation.4 | loop fusion | flops 2097152 | bytes 8388608 | tf_op jit(solution)/shard_map/concatenate | solution.py:91
  210.6 4.2 %gather_fusion.2 = bf16[4,2,256,512]{3,2,1,0:T(8,128)(2,1)} fusion(bf16[2,8,256,512]{3,2,1,0:T(8,128)(2,1)} %pad_maximum_fusion, s32[1024]{0:T(1024)S(1)} %pad_clamp_fusion.1), kind=kCustom, calls=%fused_computation.2 | custom fusion | bytes 4194320 | tf_op jit(solution)/shard_map/gather | solution.py:94
  214.8 2.7 fusion.25
  217.5 1.3 copy.32
  218.8 1.5 copy.30
  220.3 0.3 select_reduce_fusion
  220.7 0.2 bitcast_reduce_fusion
  220.9 1.6 fusion
  222.5 0.6 convert_element_type.68
  223.2 6.4 %all-to-all-start = ((bf16[2,2,4096]{2,1,0:T(2,128)(2,1)}), bf16[2,2,4096]{2,1,0:T(2,128)(2,1)S(1)}, u32[]{:S(2)}, u32[]{:S(2)}) async-start(bf16[2,2,4096]{2,1,0:T(2,128)(2,1)} %convert_element_type.68), calls=%async_computation | async-start | bytes 65536 | tf_op jit(solution)/shard_map/all_to_all | solution.py:97
  229.6 6.7 %all-to-all-done = bf16[2,2,4096]{2,1,0:T(2,128)(2,1)S(1)} async-done(((bf16[2,2,4096]{2,1,0:T(2,128)(2,1)}), bf16[2,2,4096]{2,1,0:T(2,128)(2,1)S(1)}, u32[]{:S(2)}, u32[]{:S(2)}) %all-to-all-start) | async-done | bytes 32800 | tf_op jit(solution)/shard_map/all_to_all | solution.py:97
  236.3 0.2 multiply_reduce_fusion.2
  236.5 0.1 fusion.18
  236.6 26.9 %gather_fusion.3 = bf16[4096,2,128]{2,1,0:T(2,128)(2,1)} fusion(bf16[2,64,128]{2,0,1:T(2,128)(2,1)S(1)} %fusion.18, s32[4096]{0:T(1024)S(1)} %broadcast_clamp_fusion), kind=kCustom, calls=%fused_computation.3 | custom fusion | bytes 4210688 | tf_op jit(solution)/shard_map/gather | solution.py:109
  263.5 1.9 copy.35
  265.4 0.7 copy.36
  266.1 58.3 %all_to_all.20 = bf16[128,2,32,128]{3,2,1,0:T(8,128)(2,1)S(1)} all-to-all(bf16[128,2,32,128]{3,2,1,0:T(8,128)(2,1)S(1)} %copy.36), channel_id=1, replica_groups=mesh['wide'=128,'head'=2] {'wide'}, dimensions={0} | all-to-all | bytes 4194304 | tf_op jit(solution)/shard_map/all_to_all | solution.py:110
  324.4 2.2 copy.37
  326.6 0.0 copy-start.15
  326.7 0.7 multiply_reduce_fusion
  327.4 0.5 copy-done.9
  327.9 0.7 multiply_reduce_fusion.1
  328.6 0.5 copy-done.1
  329.1 0.7 multiply_convert_fusion
  329.8 3.7 copy.38
  333.5 7.4 %all-to-all-start.2 = ((bf16[128,2,32,128]{3,1,2,0:T(2,128)(2,1)}), bf16[128,2,32,128]{3,1,2,0:T(2,128)(2,1)}, u32[]{:S(2)}, u32[]{:S(2)}) async-start(bf16[128,2,32,128]{3,1,2,0:T(2,128)(2,1)} %copy.38), calls=%async_computation.2 | async-start | bytes 4194304 | tf_op jit(solution)/shard_map/all_to_all | solution.py:116
  340.9 0.1 eq.15
  341.0 51.7 %all-to-all-done.2 = bf16[128,2,32,128]{3,1,2,0:T(2,128)(2,1)} async-done(((bf16[128,2,32,128]{3,1,2,0:T(2,128)(2,1)}), bf16[128,2,32,128]{3,1,2,0:T(2,128)(2,1)}, u32[]{:S(2)}, u32[]{:S(2)}) %all-to-all-start.2) | async-done | bytes 2097184 | tf_op jit(solution)/shard_map/all_to_all | solution.py:116
  392.7 1.9 copy.39
  394.6 0.4 convolution_bitcast_fusion
  395.0 0.7 fusion.9
  (39 shorter events, 0.2 us)
Async XLA Ops:
  0.0 1.6 copy-start
  3.6 8.2 %copy-start.10 = (s32[4]{0:T(128)S(1)}, s32[4]{0:T(128)}, u32[]{:S(2)}) copy-start(s32[4]{0:T(128)} %param.22) | copy-start | bytes 52
  3.6 10.1 %copy-start.5 = (bf16[4,512]{1,0:T(4,128)(2,1)S(1)}, bf16[4,512]{1,0:T(4,128)(2,1)}, u32[]{:S(2)}) copy-start(bf16[4,512]{1,0:T(4,128)(2,1)} %param.18) | copy-start | bytes 12292
  3.6 10.1 %copy-start.6 = (bf16[4,512]{1,0:T(4,128)(2,1)S(1)}, bf16[4,512]{1,0:T(4,128)(2,1)}, u32[]{:S(2)}) copy-start(bf16[4,512]{1,0:T(4,128)(2,1)} %param.19) | copy-start | bytes 12292
  3.6 10.2 %copy-start.11 = (s32[1,32]{1,0:T(1,128)S(1)}, s32[1,32]{1,0:T(1,128)}, u32[]{:S(2)}) copy-start(s32[1,32]{1,0:T(1,128)} %param.32) | copy-start | bytes 388
  3.6 10.2 %copy-start.12 = (s32[1,32]{1,0:T(1,128)S(1)}, s32[1,32]{1,0:T(1,128)}, u32[]{:S(2)}) copy-start(s32[1,32]{1,0:T(1,128)} %param.28) | copy-start | bytes 388
  3.6 201.5 %copy-start.13 = (s32[4]{0:T(128)S(1)}, s32[4]{0:T(128)}, u32[]{:S(2)}) copy-start(s32[4]{0:T(128)} %param.23) | copy-start | bytes 52
  3.7 201.5 %copy-start.3 = (bf16[4,4096]{1,0:T(4,128)(2,1)S(1)}, bf16[4,4096]{1,0:T(4,128)(2,1)}, u32[]{:S(2)}) copy-start(bf16[4,4096]{1,0:T(4,128)(2,1)} %param.17) | copy-start | bytes 98308
  6.8 199.2 %collective-permute-start.1 = (bf16[2,4,256,512]{3,2,1,0:T(8,128)(2,1)}, bf16[2,4,256,512]{3,2,1,0:T(8,128)(2,1)}, u32[]{:S(2)}, u32[]{:S(2)}) collective-permute-start(bf16[2,4,256,512]{3,2,1,0:T(8,128)(2,1)} %bitcast.2), channel_id=1, source_target_pairs={{0,2},{2,4},{4,6},{6,8},{8,10},{10,12},{12,14},{14,16},{16,18},{18... | collective-permute-start | bytes 6291464 | tf_op jit(solution)/shard_map/ppermute | solution.py:14
  11.8 193.5 %collective-permute-start = (bf16[4]{0:T(256)(128)(2,1)S(1)}, bf16[4]{0:T(256)(128)(2,1)S(1)}, u32[]{:S(2)}, u32[]{:S(2)}) collective-permute-start(bf16[4]{0:T(256)(128)(2,1)S(1)} %convert_element_type.60), channel_id=1, source_target_pairs={{0,2},{2,4},{4,6},{6,8},{8,10},{10,12},{12,14},{14,16},{16,18},{18... | collective-permute-start | bytes 32 | tf_op jit(solution)/shard_map/ppermute | solution.py:14
  220.3 16.0 %copy-start.2 = (bf16[2,8192]{1,0:T(2,128)(2,1)S(1)}, bf16[2,8192]{1,0:T(2,128)(2,1)}, u32[]{:S(2)}) copy-start(bf16[2,8192]{1,0:T(2,128)(2,1)} %param.24) | copy-start | bytes 98308
  220.3 16.2 %copy-start.4 = (f32[8192]{0:T(1024)S(1)}, f32[8192]{0:T(1024)}, u32[]{:S(2)}) copy-start(f32[8192]{0:T(1024)} %param.25) | copy-start | bytes 98308
  223.2 13.1 %all-to-all-start = ((bf16[2,2,4096]{2,1,0:T(2,128)(2,1)}), bf16[2,2,4096]{2,1,0:T(2,128)(2,1)S(1)}, u32[]{:S(2)}, u32[]{:S(2)}) async-start(bf16[2,2,4096]{2,1,0:T(2,128)(2,1)} %convert_element_type.68), calls=%async_computation | async-start | bytes 65536 | tf_op jit(solution)/shard_map/all_to_all | solution.py:97
  324.4 2.2 copy-start.8
  324.4 2.2 copy-start.14
  326.6 1.2 copy-start.9
  326.6 1.2 copy-start.15
  327.9 1.2 copy-start.1
  327.9 1.2 copy-start.7
  333.5 59.2 %all-to-all-start.2 = ((bf16[128,2,32,128]{3,1,2,0:T(2,128)(2,1)}), bf16[128,2,32,128]{3,1,2,0:T(2,128)(2,1)}, u32[]{:S(2)}, u32[]{:S(2)}) async-start(bf16[128,2,32,128]{3,1,2,0:T(2,128)(2,1)} %copy.38), calls=%async_computation.2 | async-start | bytes 4194304 | tf_op jit(solution)/shard_map/all_to_all | solution.py:116
where the time goes:
time: 396 us
  blocking collectives  249 us (63%)
  waiting for transfers between devices  58.4 us (15%)
  local copies, waits for them, and re-layouts  55.5 us (14%)
  starting transfers between devices  20.6 us (5%)
  other arithmetic  6.95 us (2%)
  matrix products  4.63 us (1%)
    all_gather x1, blocking collectives, per_device(): lax.all_gather(jnp.concatenate([gate_up_keep, down_keep], axis=1), 'wide'...  191 us
    all_to_all x1, blocking collectives, per_device(): lax.all_to_all(outgoing, 'wide', split_axis=0, concat_axis=0, tiled=True)  58.3 us
    all_to_all x1, waiting for transfers between devices, per_device(): lax.all_to_all(contrib, 'wide', split_axis=0, concat_axis=0, tiled=True)  51.7 us
    gather x2, local copies, waits for them, and re-layouts, per_device(): outgoing = jnp.swapaxes(normed_blocks[:, in_keep], 0, 1)  28.8 us
  transfers between devices with their start and end apart: 4, of which 2 were waited for; matrix products, arithmetic and copies ran while one was open for 0% of the time, Pallas kernels for 0%

commit v1 on v0

--- a/solution.py
+++ b/solution.py
@@ -99,8 +99,14 @@
     normed = (
         middle * lax.rsqrt(jnp.mean(middle * middle, axis=-1, keepdims=True) + 1e-05) * norm_gain
     ).astype(jnp.bfloat16)
-    keep_lists = lax.all_gather(
-        jnp.concatenate([gate_up_keep, down_keep], axis=1), "wide", axis=0, tiled=True
+    keep_lists = jnp.concatenate(
+        lax.all_to_all(
+            jnp.stack([jnp.concatenate([gate_up_keep, down_keep], axis=1)] * lax.axis_size("wide")),
+            "wide",
+            0,
+            0,
+        ),
+        axis=0,
     )
     keep = gate_up_keep.shape[1]
     in_keep, out_keep = (keep_lists[:, :keep], keep_lists[:, keep:])

time: 396 us -> 237 us (0.60)
  blocking collectives: 249 us -> 58.7 us
  waiting for transfers between devices: 58.4 us -> 75.2 us
  starting transfers between devices: 20.6 us -> 33.9 us
    all_gather x1 -> x0, blocking collectives: 191 us -> none  [per_device(): lax.all_gather(jnp.concatenate([gate_up_keep, down_keep], axis=1), 'wide'...]
    all_to_all x0 -> x1, starting transfers between devices: none -> 11.5 us  [per_device(): lax.all_to_all(jnp.stack([jnp.concatenate([gate_up_keep, down_keep], axis...]
    ppermute x2, waiting for transfers between devices: 0.01 us -> 9.38 us  [shifted(): return lax.ppermute(block, axis, route)]
    all_to_all x0 -> x1, waiting for transfers between devices: none -> 7.49 us  [per_device(): lax.all_to_all(jnp.stack([jnp.concatenate([gate_up_keep, down_keep], axis...]
  transfers between devices with their start and end apart: 4 -> 5, of which waited for: 2 -> 4; matrix products, arithmetic and copies ran while one was open for 0% -> 1% of each run, Pallas kernels for 0% -> 0%
where the time goes in v1:
time: 237 us; the launch traced here: 236 us
  waiting for transfers between devices  75.2 us (32%)
  blocking collectives  58.7 us (25%)
  local copies, waits for them, and re-layouts  56.2 us (24%)
  starting transfers between devices  33.9 us (14%)
  other arithmetic  6.94 us (3%)
  matrix products  4.64 us (2%)
    all_to_all x1, blocking collectives, per_device(): lax.all_to_all(outgoing, 'wide', split_axis=0, concat_axis=0, tiled=True)  58.7 us
    all_to_all x1, waiting for transfers between devices, per_device(): lax.all_to_all(contrib, 'wide', split_axis=0, concat_axis=0, tiled=True)  51.7 us
    gather x2, local copies, waits for them, and re-layouts, per_device(): outgoing = jnp.swapaxes(normed_blocks[:, in_keep], 0, 1)  28.8 us
    all_to_all x1, starting transfers between devices, per_device(): lax.all_to_all(jnp.stack([jnp.concatenate([gate_up_keep, down_keep], axis...  11.5 us
    ppermute x2, waiting for transfers between devices, shifted(): return lax.ppermute(block, axis, route)  9.38 us
    all_to_all x1, starting transfers between devices, per_device(): lax.all_to_all(attention, 'head', split_axis=0, concat_axis=1, tiled=True)  8.17 us
    all_to_all x1, waiting for transfers between devices, per_device(): lax.all_to_all(jnp.stack([jnp.concatenate([gate_up_keep, down_keep], axis...  7.49 us
    all_to_all x1, starting transfers between devices, per_device(): lax.all_to_all(contrib, 'wide', split_axis=0, concat_axis=0, tiled=True)  7.43 us
  transfers between devices with their start and end apart: 5, of which 4 were waited for; matrix products, arithmetic and copies ran while one was open for 1% of the time, Pallas kernels for 0%

profile of v1, /device:TPU:1, one launch (start us, length us, event | category | flops | bytes accessed | tf_op | source)
XLA Modules:
  0.0 236.0 jit_solution(11976552089026778066)
XLA Ops:
  0.0 0.8 compare_select_fusion.1
  0.8 0.1 reshape.103
  0.9 0.7 copy-done
  1.6 2.0 gather_fusion.1
  3.7 3.2 %copy.29 = bf16[64,2,16,512]{3,2,0,1:T(8,128)(2,1)} copy(bf16[64,2,16,512]{3,2,1,0:T(8,128)(2,1)} %gather_fusion.1) | data formatting | bytes 4194304 | tf_op jit(solution)/shard_map/gather | solution.py:88
  6.9 4.9 %collective-permute-start.1 = (bf16[2,4,256,512]{3,2,1,0:T(8,128)(2,1)}, bf16[2,4,256,512]{3,2,1,0:T(8,128)(2,1)}, u32[]{:S(2)}, u32[]{:S(2)}) collective-permute-start(bf16[2,4,256,512]{3,2,1,0:T(8,128)(2,1)} %bitcast.2), channel_id=1, source_target_pairs={{0,2},{2,4},{4,6},{6,8},{8,10},{10,12},{12,14},{14,16},{16,18},{18... | collective-permute-start | bytes 6291464 | tf_op jit(solution)/shard_map/ppermute | solution.py:14
  11.8 1.9 collective-permute-start
  13.8 0.1 add_bitcast_fusion
  13.8 0.7 stack.2
  14.5 11.5 %all-to-all-start.1 = ((s32[128,1,64]{2,1,0:T(1,128)}), s32[128,1,64]{2,1,0:T(1,128)S(1)}, u32[]{:S(2)}, u32[]{:S(2)}) async-start(s32[128,1,64]{2,1,0:T(1,128)} %stack.2), calls=%async_computation.1 | async-start | bytes 131072 | tf_op jit(solution)/shard_map/all_to_all | solution.py:103
  26.1 0.1 fusion.15
  26.2 9.4 %collective-permute-done = bf16[4]{0:T(256)(128)(2,1)S(1)} collective-permute-done((bf16[4]{0:T(256)(128)(2,1)S(1)}, bf16[4]{0:T(256)(128)(2,1)S(1)}, u32[]{:S(2)}, u32[]{:S(2)}) %collective-permute-start) | collective-permute-done | bytes 40 | tf_op jit(solution)/shard_map/ppermute | solution.py:14
  35.6 0.1 maximum_convert_fusion
  35.7 0.6 gather_fusion
  36.3 0.1 iota_compare_fusion.1
  36.4 7.5 %all-to-all-done.1 = s32[128,1,64]{2,1,0:T(1,128)S(1)} async-done(((s32[128,1,64]{2,1,0:T(1,128)}), s32[128,1,64]{2,1,0:T(1,128)S(1)}, u32[]{:S(2)}, u32[]{:S(2)}) %all-to-all-start.1) | async-done | bytes 32800 | tf_op jit(solution)/shard_map/all_to_all | solution.py:103
  43.9 0.1 fusion.26
  43.9 0.1 reshape.119
  44.0 4.5 %pad_maximum_fusion = bf16[2,8,256,512]{3,2,1,0:T(8,128)(2,1)} fusion(bf16[2,4,256,512]{3,2,1,0:T(8,128)(2,1)} %bitcast.2, bf16[2,4,256,512]{3,2,1,0:T(8,128)(2,1)} %collective-permute-done.1), kind=kLoop, calls=%fused_computation.4 | loop fusion | flops 2097152 | bytes 8388608 | tf_op jit(solution)/shard_map/concatenate | solution.py:91
  48.6 4.2 %gather_fusion.2 = bf16[4,2,256,512]{3,2,1,0:T(8,128)(2,1)} fusion(bf16[2,8,256,512]{3,2,1,0:T(8,128)(2,1)} %pad_maximum_fusion, s32[1024]{0:T(1024)S(1)} %pad_clamp_fusion.1), kind=kCustom, calls=%fused_computation.2 | custom fusion | bytes 4194320 | tf_op jit(solution)/shard_map/gather | solution.py:94
  52.8 2.7 %fusion.25 = (bf16[1,4,256,512]{3,2,0,1:T(8,128)(2,1)}, bf16[1,4,256,512]{3,2,0,1:T(8,128)(2,1)S(1)}) fusion(bf16[2,4,256,512]{3,2,0,1:T(8,128)(2,1)} %bitcast.73), kind=kLoop, calls=%fused_computation.57 | loop fusion | bytes 4194304 | tf_op jit(solution)/shard_map/slice | solution.py:23
  55.5 1.3 copy.32
  56.8 1.5 copy.30
  58.3 0.3 select_reduce_fusion
  58.6 0.2 bitcast_reduce_fusion
  58.9 1.6 fusion
  60.5 0.6 convert_element_type.68
  61.1 8.2 %all-to-all-start = ((bf16[2,2,4096]{2,1,0:T(2,128)(2,1)}), bf16[2,2,4096]{2,1,0:T(2,128)(2,1)S(1)}, u32[]{:S(2)}, u32[]{:S(2)}) async-start(bf16[2,2,4096]{2,1,0:T(2,128)(2,1)} %convert_element_type.68), calls=%async_computation | async-start | bytes 65536 | tf_op jit(solution)/shard_map/all_to_all | solution.py:97
  69.3 6.7 %all-to-all-done = bf16[2,2,4096]{2,1,0:T(2,128)(2,1)S(1)} async-done(((bf16[2,2,4096]{2,1,0:T(2,128)(2,1)}), bf16[2,2,4096]{2,1,0:T(2,128)(2,1)S(1)}, u32[]{:S(2)}, u32[]{:S(2)}) %all-to-all-start) | async-done | bytes 32800 | tf_op jit(solution)/shard_map/all_to_all | solution.py:97
  76.1 0.2 multiply_reduce_fusion.2
  76.3 0.1 fusion.18
  76.4 27.0 %gather_fusion.3 = bf16[4096,2,128]{2,1,0:T(2,128)(2,1)} fusion(bf16[2,64,128]{2,0,1:T(2,128)(2,1)S(1)} %fusion.18, s32[4096]{0:T(1024)S(1)} %broadcast_clamp_fusion), kind=kCustom, calls=%fused_computation.3 | custom fusion | bytes 4210688 | tf_op jit(solution)/shard_map/gather | solution.py:115
  103.3 1.9 copy.35
  105.2 0.7 copy.36
  105.9 58.7 %all_to_all.25 = bf16[128,2,32,128]{3,2,1,0:T(8,128)(2,1)S(1)} all-to-all(bf16[128,2,32,128]{3,2,1,0:T(8,128)(2,1)S(1)} %copy.36), channel_id=1, replica_groups=mesh['wide'=128,'head'=2] {'wide'}, dimensions={0} | all-to-all | bytes 4194304 | tf_op jit(solution)/shard_map/all_to_all | solution.py:116
  164.7 2.2 copy.37
  166.9 0.7 multiply_reduce_fusion
  167.6 0.5 copy-done.9
  168.1 0.7 multiply_reduce_fusion.1
  168.8 0.5 copy-done.1
  169.4 0.7 multiply_convert_fusion
  170.1 3.7 %copy.38 = bf16[128,2,32,128]{3,1,2,0:T(2,128)(2,1)} copy(bf16[128,2,32,128]{3,1,0,2:T(2,128)(2,1)S(1)} %bitcast.74) | data formatting | bytes 4194304 | tf_op jit(solution)/shard_map/reshape | solution.py:121
  173.8 7.4 %all-to-all-start.3 = ((bf16[128,2,32,128]{3,1,2,0:T(2,128)(2,1)}), bf16[128,2,32,128]{3,1,2,0:T(2,128)(2,1)}, u32[]{:S(2)}, u32[]{:S(2)}) async-start(bf16[128,2,32,128]{3,1,2,0:T(2,128)(2,1)} %copy.38), calls=%async_computation.3 | async-start | bytes 4194304 | tf_op jit(solution)/shard_map/all_to_all | solution.py:122
  181.2 0.1 eq.15
  181.3 51.7 %all-to-all-done.3 = bf16[128,2,32,128]{3,1,2,0:T(2,128)(2,1)} async-done(((bf16[128,2,32,128]{3,1,2,0:T(2,128)(2,1)}), bf16[128,2,32,128]{3,1,2,0:T(2,128)(2,1)}, u32[]{:S(2)}, u32[]{:S(2)}) %all-to-all-start.3) | async-done | bytes 2097184 | tf_op jit(solution)/shard_map/all_to_all | solution.py:122
  232.9 1.9 copy.39
  234.9 0.4 convolution_bitcast_fusion
  235.3 0.7 fusion.9
  (41 shorter events, 0.2 us)
Async XLA Ops:
  0.0 1.6 copy-start
  3.6 8.2 %copy-start.10 = (s32[4]{0:T(128)S(1)}, s32[4]{0:T(128)}, u32[]{:S(2)}) copy-start(s32[4]{0:T(128)} %param.22) | copy-start | bytes 52
  3.6 10.1 %copy-start.11 = (s32[1,32]{1,0:T(1,128)S(1)}, s32[1,32]{1,0:T(1,128)}, u32[]{:S(2)}) copy-start(s32[1,32]{1,0:T(1,128)} %param.32) | copy-start | bytes 388
  3.6 10.1 %copy-start.12 = (s32[1,32]{1,0:T(1,128)S(1)}, s32[1,32]{1,0:T(1,128)}, u32[]{:S(2)}) copy-start(s32[1,32]{1,0:T(1,128)} %param.28) | copy-start | bytes 388
  3.6 22.4 %copy-start.5 = (bf16[4,512]{1,0:T(4,128)(2,1)S(1)}, bf16[4,512]{1,0:T(4,128)(2,1)}, u32[]{:S(2)}) copy-start(bf16[4,512]{1,0:T(4,128)(2,1)} %param.18) | copy-start | bytes 12292
  3.6 22.4 %copy-start.6 = (bf16[4,512]{1,0:T(4,128)(2,1)S(1)}, bf16[4,512]{1,0:T(4,128)(2,1)}, u32[]{:S(2)}) copy-start(bf16[4,512]{1,0:T(4,128)(2,1)} %param.19) | copy-start | bytes 12292
  3.6 22.4 %copy-start.13 = (s32[4]{0:T(128)S(1)}, s32[4]{0:T(128)}, u32[]{:S(2)}) copy-start(s32[4]{0:T(128)} %param.23) | copy-start | bytes 52
  3.6 22.4 %copy-start.3 = (bf16[4,4096]{1,0:T(4,128)(2,1)S(1)}, bf16[4,4096]{1,0:T(4,128)(2,1)}, u32[]{:S(2)}) copy-start(bf16[4,4096]{1,0:T(4,128)(2,1)} %param.17) | copy-start | bytes 98308
  6.9 37.2 %collective-permute-start.1 = (bf16[2,4,256,512]{3,2,1,0:T(8,128)(2,1)}, bf16[2,4,256,512]{3,2,1,0:T(8,128)(2,1)}, u32[]{:S(2)}, u32[]{:S(2)}) collective-permute-start(bf16[2,4,256,512]{3,2,1,0:T(8,128)(2,1)} %bitcast.2), channel_id=1, source_target_pairs={{0,2},{2,4},{4,6},{6,8},{8,10},{10,12},{12,14},{14,16},{16,18},{18... | collective-permute-start | bytes 6291464 | tf_op jit(solution)/shard_map/ppermute | solution.py:14
  11.8 23.8 %collective-permute-start = (bf16[4]{0:T(256)(128)(2,1)S(1)}, bf16[4]{0:T(256)(128)(2,1)S(1)}, u32[]{:S(2)}, u32[]{:S(2)}) collective-permute-start(bf16[4]{0:T(256)(128)(2,1)S(1)} %convert_element_type.60), channel_id=1, source_target_pairs={{0,2},{2,4},{4,6},{6,8},{8,10},{10,12},{12,14},{14,16},{16,18},{18... | collective-permute-start | bytes 32 | tf_op jit(solution)/shard_map/ppermute | solution.py:14
  14.5 29.4 %all-to-all-start.1 = ((s32[128,1,64]{2,1,0:T(1,128)}), s32[128,1,64]{2,1,0:T(1,128)S(1)}, u32[]{:S(2)}, u32[]{:S(2)}) async-start(s32[128,1,64]{2,1,0:T(1,128)} %stack.2), calls=%async_computation.1 | async-start | bytes 131072 | tf_op jit(solution)/shard_map/all_to_all | solution.py:103
  58.3 17.8 %copy-start.2 = (bf16[2,8192]{1,0:T(2,128)(2,1)S(1)}, bf16[2,8192]{1,0:T(2,128)(2,1)}, u32[]{:S(2)}) copy-start(bf16[2,8192]{1,0:T(2,128)(2,1)} %param.24) | copy-start | bytes 98308
  58.3 18.0 %copy-start.4 = (f32[8192]{0:T(1024)S(1)}, f32[8192]{0:T(1024)}, u32[]{:S(2)}) copy-start(f32[8192]{0:T(1024)} %param.25) | copy-start | bytes 98308
  61.1 14.9 %all-to-all-start = ((bf16[2,2,4096]{2,1,0:T(2,128)(2,1)}), bf16[2,2,4096]{2,1,0:T(2,128)(2,1)S(1)}, u32[]{:S(2)}, u32[]{:S(2)}) async-start(bf16[2,2,4096]{2,1,0:T(2,128)(2,1)} %convert_element_type.68), calls=%async_computation | async-start | bytes 65536 | tf_op jit(solution)/shard_map/all_to_all | solution.py:97
  164.7 2.2 copy-start.8
  164.7 2.2 copy-start.14
  166.9 1.2 copy-start.9
  166.9 1.2 copy-start.15
  168.1 1.2 copy-start.1
  168.1 1.2 copy-start.7
  173.8 59.2 %all-to-all-start.3 = ((bf16[128,2,32,128]{3,1,2,0:T(2,128)(2,1)}), bf16[128,2,32,128]{3,1,2,0:T(2,128)(2,1)}, u32[]{:S(2)}, u32[]{:S(2)}) async-start(bf16[128,2,32,128]{3,1,2,0:T(2,128)(2,1)} %copy.38), calls=%async_computation.3 | async-start | bytes 4194304 | tf_op jit(solution)/shard_map/all_to_all | solution.py:122
